TPU v7x, 32 devices: a whole 2x2x4 slice. The times are simulated.
32 devices in a mesh: layer: 2 (over y), facet: 16 (over z, x, core).
Axes of the slice: x: 2, y: 2, z: 4, core: 2. Of those that a mesh axis runs over, the one named last changes fastest.
Arguments:
- slabs: bfloat16 [2, 2, 64, 49152], P('layer', None, None, 'facet'), may hold values from -6 to 6
- window: float32 [49152], P('facet'), may hold values from 0.5 to 1.5
- density: int32 [2, 64, 8192], P('layer', None, 'facet'), may hold values from 0 to 7
- offsets: int32 [16], replicated, may hold values from 0 to 49151
Outputs:
- image_out: float32 [2, 64, 49152], P(None, 'layer', 'facet')
All inputs are finite; a program needn't handle non-finite values.
Results may differ from a plain program's by a relative error of at most 0.0052.
Values may be sent and summed in bfloat16 or wider, within the bound.
A program may use at most 64 MiB of HBM per device.

v0:
```python
import functools
import math

import jax
import jax.numpy as jnp
from jax import lax
from jax.experimental import pallas as pl
from jax.experimental.pallas import tpu as pltpu
from jax.sharding import PartitionSpec as P

CONTRIB = 128
SUB = 512
GROUP = 4
CHUNK = 512
ROWS = 256
STEP = SUB // CONTRIB

MESH = pl.DeviceIdType.MESH


def sincos(turns, period):
    quarter = jnp.floor(turns.astype(jnp.float32) * (4.0 / period) + 0.5).astype(jnp.int32)
    rest = 4 * turns - quarter * period
    y = rest.astype(jnp.float32) * (0.5 * math.pi / period)
    z = y * y
    s = y + y * z * (-1.0 / 6 + z * (1.0 / 120 + z * (-1.0 / 5040 + z * (1.0 / 362880))))
    c = 1.0 + z * (-0.5 + z * (1.0 / 24 + z * (-1.0 / 720 + z * (1.0 / 40320))))
    odd = (quarter & 1) == 1
    cos_abs = jnp.where(odd, s, c)
    sin_abs = jnp.where(odd, c, s)
    cos_part = jnp.where(((quarter + 1) & 2) == 2, -cos_abs, cos_abs)
    sin_part = jnp.where((quarter & 2) == 2, -sin_abs, sin_abs)
    return cos_part, sin_part


def remainder(value, period):
    return value - jnp.floor(value.astype(jnp.float32) * (1.0 / period)).astype(jnp.int32) * period


def kernel(
    layers, facets, cols, width,
    slab_ref, window_ref, density_ref, offset_ref,
    out_ref,
    slab, counts_ref, window_here, offset_here, wind, ca, sa, table, modulated, acc,
    send1, recv1, embed, kr, ki, rr, ri, raw,
    send2, recv2,
    ssem1, rsem1, ssem2, rsem2, local_sem, up_sem, down_sem, layer_sem,
):
    layer = lax.axis_index("layer")
    me = lax.axis_index("facet")
    image = facets * width
    groups = facets // GROUP
    part = cols // layers
    mine = me // GROUP
    half = mine // (groups // 2)
    half_groups = groups // 2

    def outward(step):
        return jnp.where(
            half == 0,
            lax.rem(half_groups + step, groups),
            lax.rem(half_groups - 1 - step + groups, groups),
        )

    def inward(step):
        return jnp.where(half == 0, step, groups - 1 - step)

    def signal(sem, where):
        pl.semaphore_signal(sem, inc=1, device_id=where, device_id_type=MESH)

    barrier = pltpu.get_barrier_semaphore()
    for o in range(1, layers):
        signal(barrier, (lax.rem(layer + o, layers), me))
    for o in range(1, GROUP):
        signal(barrier, (layer, mine * GROUP + lax.rem(me + o, GROUP)))
    for o in range(GROUP):

        @pl.when(mine > 0)
        def _():
            signal(barrier, (layer, (mine - 1) * GROUP + lax.rem(me + o, GROUP)))

        @pl.when(mine < groups - 1)
        def _():
            signal(barrier, (layer, (mine + 1) * GROUP + lax.rem(me + o, GROUP)))

    fetch_offsets = pltpu.make_async_copy(offset_ref, offset_here, local_sem.at[3])
    fetch_offsets.start()
    fetch_window = pltpu.make_async_copy(window_ref, window_here, local_sem.at[2])
    fetch_window.start()
    fetch_slab = pltpu.make_async_copy(slab_ref, slab, local_sem.at[0])
    fetch_slab.start()
    fetch_counts = pltpu.make_async_copy(density_ref, counts_ref, local_sem.at[1])
    fetch_counts.start()

    def relay(d, wanted_up, wanted_down):
        has_up = mine + d <= groups - 1
        has_down = mine - d >= 0

        @pl.when(jnp.logical_and(has_up, wanted_up))
        def _():
            pl.semaphore_wait(up_sem.at[d], 1)
            if d + 1 < groups:

                @pl.when(mine > 0)
                def _():
                    signal(up_sem.at[d + 1], (layer, me - GROUP))

        @pl.when(jnp.logical_and(has_down, wanted_down))
        def _():
            pl.semaphore_wait(down_sem.at[d], 1)
            if d + 1 < groups:

                @pl.when(mine < groups - 1)
                def _():
                    signal(down_sem.at[d + 1], (layer, me + GROUP))

    first_up = jnp.where(half == 0, half_groups - mine, 1)
    first_down = jnp.where(half == 1, mine - half_groups + 1, 1)

    def meet_near():
        @pl.when(mine == 0)
        def _():
            pl.semaphore_wait(barrier, 2 * GROUP - 1 + layers - 1)

        @pl.when(mine == groups - 1)
        def _():
            pl.semaphore_wait(barrier, 2 * GROUP - 1 + layers - 1)

        @pl.when(jnp.logical_and(mine > 0, mine < groups - 1))
        def _():
            pl.semaphore_wait(barrier, 3 * GROUP - 1 + layers - 1)
            signal(up_sem.at[2], (layer, me - GROUP))
            signal(down_sem.at[2], (layer, me + GROUP))

        for d in range(2, groups):
            relay(d, d <= first_up, d <= first_down)

    def meet_far():
        for d in range(2, groups):
            relay(d, d > first_up, d > first_down)
        for o in range(1, layers):
            signal(layer_sem, (lax.rem(layer + o, layers), me))


    lane = lax.broadcasted_iota(jnp.int32, (ROWS, CONTRIB), 1) * STEP
    row = lax.broadcasted_iota(jnp.int32, (ROWS, CONTRIB), 0)
    base_c, base_s = sincos(remainder(lane * me, facets) * width + remainder(lane * row, image), image)
    small = lax.broadcasted_iota(jnp.int32, (8, CONTRIB), 1) * STEP
    for k in range(width // ROWS):
        rot_c, rot_s = sincos(remainder(small * (ROWS * k), image), image)
        rot_c = rot_c[0:1]
        rot_s = rot_s[0:1]
        table[k * ROWS:(k + 1) * ROWS, 0:CONTRIB] = (base_c * rot_c - base_s * rot_s).astype(jnp.bfloat16)
        table[k * ROWS:(k + 1) * ROWS, CONTRIB:2 * CONTRIB] = (
            base_c * rot_s + base_s * rot_c
        ).astype(jnp.bfloat16)

    fetch_offsets.wait()
    square = (GROUP * groups, GROUP * groups)
    on_diagonal = lax.broadcasted_iota(jnp.int32, square, 0) == lax.broadcasted_iota(jnp.int32, square, 1)
    offs = jnp.sum(
        jnp.where(on_diagonal, offset_here[...].astype(jnp.float32), 0.0), axis=1, keepdims=True
    ).astype(jnp.int32)
    start = remainder(offs * me, facets) * width
    cell = lax.broadcasted_iota(jnp.int32, (facets, width), 1)
    turns = start + remainder(offs * cell, image)
    cos_a, sin_a = sincos(turns, image)
    ca[...] = cos_a
    sa[...] = sin_a

    fetch_window.wait()
    fetch_slab.wait()
    window = window_here[...]
    for p in range(2):
        wind[p * cols:(p + 1) * cols, :] = (
            (slab[0, p].astype(jnp.float32) * window).astype(jnp.bfloat16).astype(jnp.float32)
        )

    scale1 = width ** -0.5

    def encode(step, carry):
        g = outward(step)
        for k in range(width // CHUNK):
            xs = slice(k * CHUNK, (k + 1) * CHUNK)
            for t in range(GROUP):
                s = g * GROUP + t
                c_row = ca[pl.ds(s, 1), xs]
                s_row = sa[pl.ds(s, 1), xs]
                wr = wind[0:cols, xs]
                wi = wind[cols:2 * cols, xs]
                lo = t * 2 * cols
                modulated[k % 2, lo:lo + cols, :] = (wr * c_row + wi * s_row).astype(jnp.bfloat16)
                modulated[k % 2, lo + cols:lo + 2 * cols, :] = (wi * c_row - wr * s_row).astype(jnp.bfloat16)
            prod = jnp.dot(modulated[k % 2], table[xs, :], preferred_element_type=jnp.float32)
            if k == 0:
                acc[...] = prod
            else:
                acc[...] += prod
        for t in range(GROUP):
            lo = t * 2 * cols
            pr = acc[lo:lo + cols, :]
            pi = acc[lo + cols:lo + 2 * cols, :]
            real = pr[:, :CONTRIB] + pi[:, CONTRIB:]
            imag = pi[:, :CONTRIB] - pr[:, CONTRIB:]
            send1[g * GROUP + t, 0:cols, :] = (real * scale1).astype(jnp.bfloat16)
            send1[g * GROUP + t, cols:2 * cols, :] = (imag * scale1).astype(jnp.bfloat16)

        @pl.when(step == 0)
        def _():
            meet_near()

        @pl.when(step == 1)
        def _():
            meet_far()

        for t in range(GROUP):
            s = g * GROUP + t

            @pl.when(s != me)
            def _():
                pltpu.make_async_remote_copy(
                    src_ref=send1.at[s], dst_ref=recv1.at[me],
                    send_sem=ssem1.at[s], recv_sem=rsem1.at[me],
                    device_id=(layer, s), device_id_type=MESH,
                ).start()

            @pl.when(s == me)
            def _():
                recv1[s] = send1[s]

        return carry

    lax.fori_loop(0, groups, encode, 0)

    spacing = lax.broadcasted_iota(jnp.int32, (CONTRIB, SUB), 1) - STEP * lax.broadcasted_iota(
        jnp.int32, (CONTRIB, SUB), 0
    )
    scaled = spacing.astype(jnp.float32) * (1.0 / STEP)
    weight_k = 1.0 / (1.0 + scaled * scaled)
    c0, s0 = sincos(spacing, 2 * facets)
    kr[...] = c0 * weight_k
    ki[...] = s0 * weight_k
    c1, s1 = sincos(spacing, facets)
    rr[...] = c1
    ri[...] = s1

    def make_embed(f, carry):
        r = kr[...]
        i = ki[...]
        lo = pl.multiple_of(f * CONTRIB, CONTRIB)
        embed[pl.ds(lo, CONTRIB), 0:SUB] = r.astype(jnp.bfloat16)
        embed[pl.ds(lo, CONTRIB), SUB:2 * SUB] = (-i).astype(jnp.bfloat16)
        a = rr[...]
        b = ri[...]
        kr[...] = r * a - i * b
        ki[...] = r * b + i * a
        return carry

    lax.fori_loop(0, facets, make_embed, 0)
    raw[...] = jnp.zeros_like(raw)

    def gather(step, carry):
        g = inward(step)
        for t in range(GROUP):
            f = g * GROUP + t

            @pl.when(f != me)
            def _():
                pltpu.make_async_remote_copy(
                    src_ref=send1.at[f], dst_ref=recv1.at[f],
                    send_sem=ssem1.at[f], recv_sem=rsem1.at[f],
                    device_id=(layer, f), device_id_type=MESH,
                ).wait()

        lhs = jnp.concatenate([recv1[g * GROUP + t] for t in range(GROUP)], axis=1)
        lo = pl.multiple_of(g * GROUP * CONTRIB, GROUP * CONTRIB)
        raw[...] += jnp.dot(
            lhs, embed[pl.ds(lo, GROUP * CONTRIB), :], preferred_element_type=jnp.float32
        )
        return carry

    lax.fori_loop(0, groups, gather, 0)

    fetch_counts.wait()
    counts = counts_ref[0]
    weights = jnp.where(
        counts > 0, 1.0 / jnp.maximum(counts, 1).astype(jnp.float32), 0.0
    )
    sub_scale = (2 * facets) ** -0.5
    raw_r = raw[0:cols, 0:SUB] - raw[cols:2 * cols, SUB:2 * SUB]
    raw_i = raw[0:cols, SUB:2 * SUB] + raw[cols:2 * cols, 0:SUB]
    gridded = jnp.concatenate(
        [
            (raw_r * weights * sub_scale).astype(jnp.bfloat16),
            (raw_i * weights * sub_scale).astype(jnp.bfloat16),
        ],
        axis=0,
    )
    dims = (((1,), (1,)), ((), ()))

    pl.semaphore_wait(layer_sem, layers - 1)

    def scatter(step, carry):
        g = outward(step)
        lo = pl.multiple_of(g * GROUP * CONTRIB, GROUP * CONTRIB)
        er = embed[pl.ds(lo, GROUP * CONTRIB), 0:SUB]
        ei = embed[pl.ds(lo, GROUP * CONTRIB), SUB:2 * SUB]
        pr = lax.dot_general(gridded, er, dims, preferred_element_type=jnp.float32)
        pi = lax.dot_general(gridded, ei, dims, preferred_element_type=jnp.float32)
        real = ((pr[0:cols] + pi[cols:2 * cols]) * 0.5).astype(jnp.bfloat16)
        imag = ((pr[cols:2 * cols] - pi[0:cols]) * 0.5).astype(jnp.bfloat16)
        for t in range(GROUP):
            f = g * GROUP + t
            js = slice(t * CONTRIB, (t + 1) * CONTRIB)
            for l in range(layers):
                send2[f, l, 0] = real[l * part:(l + 1) * part, js]
                send2[f, l, 1] = imag[l * part:(l + 1) * part, js]
        for t in range(GROUP):
            f = g * GROUP + t
            for l in range(layers):
                own = jnp.logical_and(f == me, layer == l)

                @pl.when(jnp.logical_not(own))
                def _():
                    pltpu.make_async_remote_copy(
                        src_ref=send2.at[f, l], dst_ref=recv2.at[layer, me],
                        send_sem=ssem2.at[l, f], recv_sem=rsem2.at[layer, me],
                        device_id=(l, f), device_id_type=MESH,
                    ).start()

                @pl.when(own)
                def _():
                    recv2[layer, me] = send2[f, l]

        return carry

    lax.fori_loop(0, groups, scatter, 0)

    out_ref[...] = jnp.zeros_like(out_ref)
    out_scale = (facets * CONTRIB) ** -0.5

    def adjoint(step, carry):
        g = inward(step)
        tops = []
        for t in range(GROUP):
            s = g * GROUP + t
            for l in range(layers):
                own = jnp.logical_and(s == me, layer == l)

                @pl.when(jnp.logical_not(own))
                def _():
                    pltpu.make_async_remote_copy(
                        src_ref=send2.at[s, l], dst_ref=recv2.at[l, s],
                        send_sem=ssem2.at[l, s], recv_sem=rsem2.at[l, s],
                        device_id=(l, s), device_id_type=MESH,
                    ).wait()

        for t in range(GROUP):
            s = g * GROUP + t
            br = recv2[0, s, 0].astype(jnp.float32)
            bi = recv2[0, s, 1].astype(jnp.float32)
            for l in range(1, layers):
                br = br + recv2[l, s, 0].astype(jnp.float32)
                bi = bi + recv2[l, s, 1].astype(jnp.float32)
            tops.append(jnp.concatenate([br, -bi], axis=1))
            tops.append(jnp.concatenate([bi, br], axis=1))
        lhs = jnp.concatenate(tops, axis=0).astype(jnp.bfloat16)
        for k in range(width // CHUNK):
            xs = slice(k * CHUNK, (k + 1) * CHUNK)
            prod = lax.dot_general(lhs, table[xs, :], dims, preferred_element_type=jnp.float32)
            out_r = out_ref[0, :, xs]
            out_i = out_ref[1, :, xs]
            for t in range(GROUP):
                s = g * GROUP + t
                c_row = ca[pl.ds(s, 1), xs]
                s_row = sa[pl.ds(s, 1), xs]
                gr = prod[(2 * t) * part:(2 * t + 1) * part]
                gi = prod[(2 * t + 1) * part:(2 * t + 2) * part]
                out_r = out_r + (c_row * gr - s_row * gi)
                out_i = out_i + (c_row * gi + s_row * gr)
            factor = jnp.where(step == groups - 1, window_here[:, xs] * out_scale, 1.0)
            out_ref[0, :, xs] = out_r * factor
            out_ref[1, :, xs] = out_i * factor
        return carry

    lax.fori_loop(0, groups, adjoint, 0)


def shards(slabs, window, density, offsets):
    facets = lax.axis_size("facet")
    layers = lax.axis_size("layer")
    cols = slabs.shape[2]
    width = slabs.shape[3]
    part = cols // layers
    f32, bf16 = jnp.float32, jnp.bfloat16
    summed = pl.pallas_call(
        functools.partial(kernel, layers, facets, cols, width),
        out_shape=jax.ShapeDtypeStruct((2, part, width), f32),
        in_specs=[pl.BlockSpec(memory_space=pltpu.HBM)] * 4,
        out_specs=pl.BlockSpec(memory_space=pltpu.VMEM),
        scratch_shapes=[
            pltpu.VMEM(slabs.shape, bf16),
            pltpu.VMEM(density.shape, jnp.int32),
            pltpu.VMEM((1, width), f32),
            pltpu.VMEM((1, facets), jnp.int32),
            pltpu.VMEM((2 * cols, width), f32),
            pltpu.VMEM((facets, width), f32),
            pltpu.VMEM((facets, width), f32),
            pltpu.VMEM((width, 2 * CONTRIB), bf16),
            pltpu.VMEM((2, GROUP * 2 * cols, CHUNK), bf16),
            pltpu.VMEM((GROUP * 2 * cols, 2 * CONTRIB), f32),
            pltpu.VMEM((facets, 2 * cols, CONTRIB), bf16),
            pltpu.VMEM((facets, 2 * cols, CONTRIB), bf16),
            pltpu.VMEM((facets * CONTRIB, 2 * SUB), bf16),
            pltpu.VMEM((CONTRIB, SUB), f32),
            pltpu.VMEM((CONTRIB, SUB), f32),
            pltpu.VMEM((CONTRIB, SUB), f32),
            pltpu.VMEM((CONTRIB, SUB), f32),
            pltpu.VMEM((2 * cols, 2 * SUB), f32),
            pltpu.VMEM((facets, layers, 2, part, CONTRIB), bf16),
            pltpu.VMEM((layers, facets, 2, part, CONTRIB), bf16),
            pltpu.SemaphoreType.DMA((facets,)),
            pltpu.SemaphoreType.DMA((facets,)),
            pltpu.SemaphoreType.DMA((layers, facets)),
            pltpu.SemaphoreType.DMA((layers, facets)),
            pltpu.SemaphoreType.DMA((4,)),
            pltpu.SemaphoreType.REGULAR((facets // GROUP,)),
            pltpu.SemaphoreType.REGULAR((facets // GROUP,)),
            pltpu.SemaphoreType.REGULAR,
        ],
        compiler_params=pltpu.CompilerParams(
            collective_id=0, has_side_effects=True, vmem_limit_bytes=(14 + facets) * 1024 * 1024
        ),
    )(
        *(
            pltpu.with_memory_space_constraint(x, pltpu.HBM)
            for x in (slabs, window[None, :], density, offsets[None, :])
        )
    )
    return summed


def solution(mesh):
    placed = (P("layer", None, None, "facet"), P("facet"), P("layer", None, "facet"), P())
    return jax.shard_map(
        shards, mesh=mesh, in_specs=placed, out_specs=P(None, "layer", "facet"), check_vma=False
    )
```

profile of v0, /device:TPU:0, one launch (start us, length us, event | category | flops | bytes accessed | tf_op | source)
XLA Modules:
  0.0 34.9 jit_solution(17539739321278223189)
XLA Ops:
  0.0 34.0 %shard_map.46 = f32[2,32,3072]{2,1,0:T(8,128)S(1)} custom-call(bf16[1,2,64,3072]{3,2,1,0:T(8,128)(2,1)} %slab_ref.1, f32[1,3072]{1,0:T(1,128)} %bitcast.2, s32[1,64,512]{2,1,0:T(8,128)} %density_ref.1, s32[1,16]{1,0:T(1,128)} %bitcast.3), custom_call_target="tpu_custom_call" | custom-call | tf_op jit(solution)/shard_map/pallas_call | solution.py:396
  34.0 0.9 %copy.6 = f32[2,32,3072]{2,1,0:T(8,128)} copy(f32[2,32,3072]{2,1,0:T(8,128)S(1)} %shard_map.46) | data formatting | bytes 1572864
where the time goes:
time: 35.1 us; the launch traced here: 34.9 us
  Pallas kernels  34 us (97%)
  local copies, waits for them, and re-layouts  0.88 us (3%)
    pallas_call x1, Pallas kernels, shards(): pl.pallas_call(functools.partial(kernel, layers, facets, cols, width), ou...  34 us
    unnamed x1, local copies, waits for them, and re-layouts  0.88 us

commit v1 on v0

v1 whole, which is shorter than its diff:
```python
import functools
import math

import jax
import jax.numpy as jnp
from jax import lax
from jax.experimental import pallas as pl
from jax.experimental.pallas import tpu as pltpu
from jax.sharding import PartitionSpec as P

CONTRIB = 128
SUB = 512
GROUP = 4
CHUNK = 512
ROWS = 256
STEP = SUB // CONTRIB
CHUNKS = 2

MESH = pl.DeviceIdType.MESH


def sincos(turns, period):
    quarter = jnp.floor(turns.astype(jnp.float32) * (4.0 / period) + 0.5).astype(jnp.int32)
    rest = 4 * turns - quarter * period
    y = rest.astype(jnp.float32) * (0.5 * math.pi / period)
    z = y * y
    s = y + y * z * (-1.0 / 6 + z * (1.0 / 120 + z * (-1.0 / 5040 + z * (1.0 / 362880))))
    c = 1.0 + z * (-0.5 + z * (1.0 / 24 + z * (-1.0 / 720 + z * (1.0 / 40320))))
    odd = (quarter & 1) == 1
    cos_abs = jnp.where(odd, s, c)
    sin_abs = jnp.where(odd, c, s)
    cos_part = jnp.where(((quarter + 1) & 2) == 2, -cos_abs, cos_abs)
    sin_part = jnp.where((quarter & 2) == 2, -sin_abs, sin_abs)
    return cos_part, sin_part


def remainder(value, period):
    return value - jnp.floor(value.astype(jnp.float32) * (1.0 / period)).astype(jnp.int32) * period


def kernel(
    layers, facets, cols, width, chunks,
    slab_ref, window_ref, density_ref, offset_ref,
    out_ref,
    slab, counts, window_here, offset_here, wind, ca, sa, table, modulated, acc,
    send1, recv1, embed, kr, ki, rr, ri, raw,
    send2, recv2,
    ssem1, rsem1, ssem2, rsem2, csem, local_sem, up_sem, down_sem,
):
    layer = lax.axis_index("layer")
    me = lax.axis_index("facet")
    image = facets * width
    groups = facets // GROUP
    part = cols // layers
    wide = part // chunks
    band = layers * wide
    mine = me // GROUP
    half = mine // (groups // 2)
    half_groups = groups // 2

    def outward(step):
        return jnp.where(
            half == 0,
            lax.rem(half_groups + step, groups),
            lax.rem(half_groups - 1 - step + groups, groups),
        )

    def inward(step):
        return jnp.where(half == 0, step, groups - 1 - step)

    def signal(sem, where):
        pl.semaphore_signal(sem, inc=1, device_id=where, device_id_type=MESH)

    barrier = pltpu.get_barrier_semaphore()
    for l in range(layers):
        there = lax.rem(layer + l, layers)
        for o in range(GROUP):
            if l > 0 or o > 0:
                signal(barrier, (there, mine * GROUP + lax.rem(me + o, GROUP)))

            @pl.when(mine > 0)
            def _():
                signal(barrier, (there, (mine - 1) * GROUP + lax.rem(me + o, GROUP)))

            @pl.when(mine < groups - 1)
            def _():
                signal(barrier, (there, (mine + 1) * GROUP + lax.rem(me + o, GROUP)))

    fetch_offsets = pltpu.make_async_copy(offset_ref, offset_here, local_sem.at[2])
    fetch_offsets.start()
    fetch_window = pltpu.make_async_copy(window_ref, window_here, local_sem.at[1])
    fetch_window.start()
    fetch_slab = pltpu.make_async_copy(slab_ref, slab, local_sem.at[0])
    fetch_slab.start()

    def relay(d, wanted_up, wanted_down):
        has_up = mine + d <= groups - 1
        has_down = mine - d >= 0

        @pl.when(jnp.logical_and(has_up, wanted_up))
        def _():
            pl.semaphore_wait(up_sem.at[d], 1)
            if d + 1 < groups:

                @pl.when(mine > 0)
                def _():
                    signal(up_sem.at[d + 1], (layer, me - GROUP))

        @pl.when(jnp.logical_and(has_down, wanted_down))
        def _():
            pl.semaphore_wait(down_sem.at[d], 1)
            if d + 1 < groups:

                @pl.when(mine < groups - 1)
                def _():
                    signal(down_sem.at[d + 1], (layer, me + GROUP))

    first_up = jnp.where(half == 0, half_groups - mine, 1)
    first_down = jnp.where(half == 1, mine - half_groups + 1, 1)

    def meet_near():
        at_end = jnp.logical_or(mine == 0, mine == groups - 1)

        @pl.when(at_end)
        def _():
            pl.semaphore_wait(barrier, 2 * GROUP * layers - 1)

        @pl.when(jnp.logical_not(at_end))
        def _():
            pl.semaphore_wait(barrier, 3 * GROUP * layers - 1)
            signal(up_sem.at[2], (layer, me - GROUP))
            signal(down_sem.at[2], (layer, me + GROUP))

    def meet_first():
        for d in range(2, groups):
            relay(d, d <= first_up, d <= first_down)

    def meet_far():
        for d in range(2, groups):
            relay(d, d > first_up, d > first_down)

    lane = lax.broadcasted_iota(jnp.int32, (ROWS, CONTRIB), 1) * STEP
    row = lax.broadcasted_iota(jnp.int32, (ROWS, CONTRIB), 0)
    base_c, base_s = sincos(remainder(lane * me, facets) * width + remainder(lane * row, image), image)
    small = lax.broadcasted_iota(jnp.int32, (8, CONTRIB), 1) * STEP
    for k in range(width // ROWS):
        rot_c, rot_s = sincos(remainder(small * (ROWS * k), image), image)
        rot_c = rot_c[0:1]
        rot_s = rot_s[0:1]
        table[k * ROWS:(k + 1) * ROWS, 0:CONTRIB] = (base_c * rot_c - base_s * rot_s).astype(jnp.bfloat16)
        table[k * ROWS:(k + 1) * ROWS, CONTRIB:2 * CONTRIB] = (
            base_c * rot_s + base_s * rot_c
        ).astype(jnp.bfloat16)

    fetch_offsets.wait()
    square = (GROUP * groups, GROUP * groups)
    on_diagonal = lax.broadcasted_iota(jnp.int32, square, 0) == lax.broadcasted_iota(jnp.int32, square, 1)
    offs = jnp.sum(
        jnp.where(on_diagonal, offset_here[...].astype(jnp.float32), 0.0), axis=1, keepdims=True
    ).astype(jnp.int32)
    start = remainder(offs * me, facets) * width
    cell = lax.broadcasted_iota(jnp.int32, (facets, width), 1)
    turns = start + remainder(offs * cell, image)
    cos_a, sin_a = sincos(turns, image)
    ca[...] = cos_a
    sa[...] = sin_a

    fetch_window.wait()
    fetch_slab.wait()
    window = window_here[...]
    for p in range(2):
        whole = (slab[0, p].astype(jnp.float32) * window).astype(jnp.bfloat16).astype(jnp.float32)
        for q in range(chunks):
            for h in range(layers):
                at = h * part + q * wide
                wind[q, p * band + h * wide:p * band + (h + 1) * wide, :] = whole[at:at + wide]

    meet_near()
    for l in range(layers):

        @pl.when(layer == l)
        def _():
            pltpu.make_async_copy(
                density_ref.at[0, l * part:(l + 1) * part], counts.at[l], csem.at[layers]
            ).start()

        @pl.when(layer != l)
        def _():
            pltpu.make_async_remote_copy(
                src_ref=density_ref.at[0, l * part:(l + 1) * part], dst_ref=counts.at[layer],
                send_sem=csem.at[l], recv_sem=csem.at[layers],
                device_id=(l, me), device_id_type=MESH,
            ).start()

    scale1 = width ** -0.5

    def encode(turn, carry):
        q = turn // groups
        step = lax.rem(turn, groups)
        g = outward(step)
        for k in range(width // CHUNK):
            xs = slice(k * CHUNK, (k + 1) * CHUNK)
            for t in range(GROUP):
                s = g * GROUP + t
                c_row = ca[pl.ds(s, 1), xs]
                s_row = sa[pl.ds(s, 1), xs]
                wr = wind[q, 0:band, xs]
                wi = wind[q, band:2 * band, xs]
                lo = t * 2 * band
                modulated[k % 2, lo:lo + band, :] = (wr * c_row + wi * s_row).astype(jnp.bfloat16)
                modulated[k % 2, lo + band:lo + 2 * band, :] = (wi * c_row - wr * s_row).astype(jnp.bfloat16)
            prod = jnp.dot(modulated[k % 2], table[xs, :], preferred_element_type=jnp.float32)
            if k == 0:
                acc[...] = prod
            else:
                acc[...] += prod
        for t in range(GROUP):
            lo = t * 2 * band
            pr = acc[lo:lo + band, :]
            pi = acc[lo + band:lo + 2 * band, :]
            real = (pr[:, :CONTRIB] + pi[:, CONTRIB:]) * scale1
            imag = (pi[:, :CONTRIB] - pr[:, CONTRIB:]) * scale1
            for h in range(layers):
                hs = slice(h * wide, (h + 1) * wide)
                send1[q, g * GROUP + t, h] = jnp.concatenate([real[hs], imag[hs]], axis=0).astype(jnp.bfloat16)

        @pl.when(turn == 0)
        def _():
            meet_first()

        @pl.when(turn == 1)
        def _():
            meet_far()

        for t in range(GROUP):
            s = g * GROUP + t
            for h in range(layers):
                own = jnp.logical_and(s == me, layer == h)

                @pl.when(jnp.logical_not(own))
                def _():
                    pltpu.make_async_remote_copy(
                        src_ref=send1.at[q, s, h], dst_ref=recv1.at[q, me, layer],
                        send_sem=ssem1.at[q, s, h], recv_sem=rsem1.at[q, mine],
                        device_id=(h, s), device_id_type=MESH,
                    ).start()

                @pl.when(own)
                def _():
                    pltpu.make_async_copy(
                        send1.at[q, s, h], recv1.at[q, me, layer], rsem1.at[q, mine]
                    ).start()

        return carry

    lax.fori_loop(0, chunks * groups, encode, 0)

    spacing = lax.broadcasted_iota(jnp.int32, (CONTRIB, SUB), 1) - STEP * lax.broadcasted_iota(
        jnp.int32, (CONTRIB, SUB), 0
    )
    scaled = spacing.astype(jnp.float32) * (1.0 / STEP)
    weight_k = 1.0 / (1.0 + scaled * scaled)
    c0, s0 = sincos(spacing, 2 * facets)
    kr[...] = c0 * weight_k
    ki[...] = s0 * weight_k
    c1, s1 = sincos(spacing, facets)
    rr[...] = c1
    ri[...] = s1

    def make_embed(f, carry):
        r = kr[...]
        i = ki[...]
        lo = pl.multiple_of(f * CONTRIB, CONTRIB)
        embed[pl.ds(lo, CONTRIB), 0:SUB] = r.astype(jnp.bfloat16)
        embed[pl.ds(lo, CONTRIB), SUB:2 * SUB] = (-i).astype(jnp.bfloat16)
        a = rr[...]
        b = ri[...]
        kr[...] = r * a - i * b
        ki[...] = r * b + i * a
        return carry

    lax.fori_loop(0, facets, make_embed, 0)

    pltpu.make_async_copy(counts, counts, csem.at[layers]).wait()
    sub_scale = (2 * facets) ** -0.5
    dims = (((1,), (1,)), ((), ()))

    def middle(q, carry):
        raw[...] = jnp.zeros_like(raw)

        def gather(step, inner):
            g = inward(step)
            piece = recv1.at[q, pl.ds(g * GROUP, GROUP)]
            pltpu.make_async_copy(piece, piece, rsem1.at[q, g]).wait()
            lhs = jnp.concatenate(
                [recv1[q, g * GROUP + t].reshape(2 * band, CONTRIB) for t in range(GROUP)], axis=1
            )
            lo = pl.multiple_of(g * GROUP * CONTRIB, GROUP * CONTRIB)
            raw[...] += jnp.dot(
                lhs, embed[pl.ds(lo, GROUP * CONTRIB), :], preferred_element_type=jnp.float32
            )
            return inner

        lax.fori_loop(0, groups, gather, 0)

        total_r = jnp.zeros((wide, SUB), jnp.float32)
        total_i = jnp.zeros((wide, SUB), jnp.float32)
        for l in range(layers):
            here = counts[l, pl.ds(pl.multiple_of(q * wide, wide), wide), :]
            weights = jnp.where(
                here > 0, 1.0 / jnp.maximum(here, 1).astype(jnp.float32), 0.0
            )
            re = slice(2 * l * wide, (2 * l + 1) * wide)
            im = slice((2 * l + 1) * wide, (2 * l + 2) * wide)
            raw_r = raw[re, 0:SUB] - raw[im, SUB:2 * SUB]
            raw_i = raw[re, SUB:2 * SUB] + raw[im, 0:SUB]
            total_r += (raw_r * weights * sub_scale).astype(jnp.bfloat16).astype(jnp.float32)
            total_i += (raw_i * weights * sub_scale).astype(jnp.bfloat16).astype(jnp.float32)
        gridded = jnp.concatenate([total_r, total_i], axis=0).astype(jnp.bfloat16)

        def scatter(step, inner):
            g = outward(step)
            lo = pl.multiple_of(g * GROUP * CONTRIB, GROUP * CONTRIB)
            er = embed[pl.ds(lo, GROUP * CONTRIB), 0:SUB]
            ei = embed[pl.ds(lo, GROUP * CONTRIB), SUB:2 * SUB]
            pr = lax.dot_general(gridded, er, dims, preferred_element_type=jnp.float32)
            pi = lax.dot_general(gridded, ei, dims, preferred_element_type=jnp.float32)
            real = (pr[0:wide] + pi[wide:2 * wide]) * 0.5
            imag = (pr[wide:2 * wide] - pi[0:wide]) * 0.5
            both = jnp.concatenate([real, imag], axis=0).astype(jnp.bfloat16)
            for t in range(GROUP):
                send2[q, g * GROUP + t] = both[:, t * CONTRIB:(t + 1) * CONTRIB]
            for t in range(GROUP):
                f = g * GROUP + t

                @pl.when(f != me)
                def _():
                    pltpu.make_async_remote_copy(
                        src_ref=send2.at[q, f], dst_ref=recv2.at[q, me],
                        send_sem=ssem2.at[q, f], recv_sem=rsem2.at[q, mine],
                        device_id=(layer, f), device_id_type=MESH,
                    ).start()

                @pl.when(f == me)
                def _():
                    pltpu.make_async_copy(send2.at[q, f], recv2.at[q, me], rsem2.at[q, mine]).start()

            return inner

        lax.fori_loop(0, groups, scatter, 0)
        return carry

    lax.fori_loop(0, chunks, middle, 0)

    out_ref[...] = jnp.zeros_like(out_ref)
    out_scale = (facets * CONTRIB) ** -0.5

    def adjoint(turn, carry):
        q = turn // groups
        step = lax.rem(turn, groups)
        g = inward(step)
        piece = recv2.at[q, pl.ds(g * GROUP, GROUP)]
        pltpu.make_async_copy(piece, piece, rsem2.at[q, g]).wait()
        tops = []
        for t in range(GROUP):
            both = recv2[q, g * GROUP + t].astype(jnp.float32)
            br = both[0:wide]
            bi = both[wide:2 * wide]
            tops.append(jnp.concatenate([br, -bi], axis=1))
            tops.append(jnp.concatenate([bi, br], axis=1))
        lhs = jnp.concatenate(tops, axis=0).astype(jnp.bfloat16)
        rows = pl.ds(pl.multiple_of(q * wide, wide), wide)
        for k in range(width // CHUNK):
            xs = slice(k * CHUNK, (k + 1) * CHUNK)
            prod = lax.dot_general(lhs, table[xs, :], dims, preferred_element_type=jnp.float32)
            out_r = out_ref[0, rows, xs]
            out_i = out_ref[1, rows, xs]
            for t in range(GROUP):
                s = g * GROUP + t
                c_row = ca[pl.ds(s, 1), xs]
                s_row = sa[pl.ds(s, 1), xs]
                gr = prod[(2 * t) * wide:(2 * t + 1) * wide]
                gi = prod[(2 * t + 1) * wide:(2 * t + 2) * wide]
                out_r = out_r + (c_row * gr - s_row * gi)
                out_i = out_i + (c_row * gi + s_row * gr)
            factor = jnp.where(step == groups - 1, window_here[:, xs] * out_scale, 1.0)
            out_ref[0, rows, xs] = out_r * factor
            out_ref[1, rows, xs] = out_i * factor
        return carry

    lax.fori_loop(0, chunks * groups, adjoint, 0)

    def drain(turn, carry):
        q = turn // facets
        s = lax.rem(turn, facets)
        for h in range(layers):

            @pl.when(jnp.logical_not(jnp.logical_and(s == me, layer == h)))
            def _():
                pltpu.make_async_remote_copy(
                    src_ref=send1.at[q, s, h], dst_ref=recv1.at[q, s, h],
                    send_sem=ssem1.at[q, s, h], recv_sem=rsem1.at[q, mine],
                    device_id=(h, s), device_id_type=MESH,
                ).wait_send()

        @pl.when(s != me)
        def _():
            pltpu.make_async_remote_copy(
                src_ref=send2.at[q, s], dst_ref=recv2.at[q, s],
                send_sem=ssem2.at[q, s], recv_sem=rsem2.at[q, mine],
                device_id=(layer, s), device_id_type=MESH,
            ).wait_send()

        return carry

    lax.fori_loop(0, chunks * facets, drain, 0)
    for l in range(layers):

        @pl.when(layer != l)
        def _():
            pltpu.make_async_remote_copy(
                src_ref=density_ref.at[0, l * part:(l + 1) * part], dst_ref=counts.at[l],
                send_sem=csem.at[l], recv_sem=csem.at[layers],
                device_id=(l, me), device_id_type=MESH,
            ).wait_send()


def shards(slabs, window, density, offsets):
    facets = lax.axis_size("facet")
    layers = lax.axis_size("layer")
    cols = slabs.shape[2]
    width = slabs.shape[3]
    part = cols // layers
    chunks = CHUNKS if part % (16 * CHUNKS) == 0 else 1
    wide = part // chunks
    f32, bf16 = jnp.float32, jnp.bfloat16
    summed = pl.pallas_call(
        functools.partial(kernel, layers, facets, cols, width, chunks),
        out_shape=jax.ShapeDtypeStruct((2, part, width), f32),
        in_specs=[pl.BlockSpec(memory_space=pltpu.HBM)] * 4,
        out_specs=pl.BlockSpec(memory_space=pltpu.VMEM),
        scratch_shapes=[
            pltpu.VMEM(slabs.shape, bf16),
            pltpu.VMEM((layers, part, SUB), jnp.int32),
            pltpu.VMEM((1, width), f32),
            pltpu.VMEM((1, facets), jnp.int32),
            pltpu.VMEM((chunks, 2 * layers * wide, width), f32),
            pltpu.VMEM((facets, width), f32),
            pltpu.VMEM((facets, width), f32),
            pltpu.VMEM((width, 2 * CONTRIB), bf16),
            pltpu.VMEM((2, GROUP * 2 * layers * wide, CHUNK), bf16),
            pltpu.VMEM((GROUP * 2 * layers * wide, 2 * CONTRIB), f32),
            pltpu.VMEM((chunks, facets, layers, 2 * wide, CONTRIB), bf16),
            pltpu.VMEM((chunks, facets, layers, 2 * wide, CONTRIB), bf16),
            pltpu.VMEM((facets * CONTRIB, 2 * SUB), bf16),
            pltpu.VMEM((CONTRIB, SUB), f32),
            pltpu.VMEM((CONTRIB, SUB), f32),
            pltpu.VMEM((CONTRIB, SUB), f32),
            pltpu.VMEM((CONTRIB, SUB), f32),
            pltpu.VMEM((2 * layers * wide, 2 * SUB), f32),
            pltpu.VMEM((chunks, facets, 2 * wide, CONTRIB), bf16),
            pltpu.VMEM((chunks, facets, 2 * wide, CONTRIB), bf16),
            pltpu.SemaphoreType.DMA((chunks, facets, layers)),
            pltpu.SemaphoreType.DMA((chunks, facets // GROUP)),
            pltpu.SemaphoreType.DMA((chunks, facets)),
            pltpu.SemaphoreType.DMA((chunks, facets // GROUP)),
            pltpu.SemaphoreType.DMA((layers + 1,)),
            pltpu.SemaphoreType.DMA((3,)),
            pltpu.SemaphoreType.REGULAR((facets // GROUP,)),
            pltpu.SemaphoreType.REGULAR((facets // GROUP,)),
        ],
        compiler_params=pltpu.CompilerParams(
            collective_id=0, has_side_effects=True, vmem_limit_bytes=(14 + facets) * 1024 * 1024
        ),
    )(
        *(
            pltpu.with_memory_space_constraint(x, pltpu.HBM)
            for x in (slabs, window[None, :], density, offsets[None, :])
        )
    )
    return summed


def solution(mesh):
    placed = (P("layer", None, None, "facet"), P("facet"), P("layer", None, "facet"), P())
    return jax.shard_map(
        shards, mesh=mesh, in_specs=placed, out_specs=P(None, "layer", "facet"), check_vma=False
    )
```

time: 35.1 us -> 32.3 us (0.920)
  Pallas kernels: 34 us -> 31.3 us
    pallas_call x1, Pallas kernels: 34 us -> 31.3 us  [shards(): pl.pallas_call(functools.partial(kernel, layers, facets, cols, width, chu...]
where the time goes in v1:
time: 32.3 us; the launch traced here: 32.2 us
  Pallas kernels  31.3 us (97%)
  local copies, waits for them, and re-layouts  0.88 us (3%)
    pallas_call x1, Pallas kernels, shards(): pl.pallas_call(functools.partial(kernel, layers, facets, cols, width, chu...  31.3 us
    unnamed x1, local copies, waits for them, and re-layouts  0.88 us

profile of v1, /device:TPU:0, one launch (start us, length us, event | category | flops | bytes accessed | tf_op | source)
XLA Modules:
  0.0 32.2 jit_solution(1361452920649714743)
XLA Ops:
  0.0 31.3 %shard_map.46 = f32[2,32,3072]{2,1,0:T(8,128)S(1)} custom-call(bf16[1,2,64,3072]{3,2,1,0:T(8,128)(2,1)} %slab_ref.1, f32[1,3072]{1,0:T(1,128)} %bitcast.2, s32[1,64,512]{2,1,0:T(8,128)} %density_ref.1, s32[1,16]{1,0:T(1,128)} %bitcast.3), custom_call_target="tpu_custom_call" | custom-call | tf_op jit(solution)/shard_map/pallas_call | solution.py:437
  31.3 0.9 %copy.6 = f32[2,32,3072]{2,1,0:T(8,128)} copy(f32[2,32,3072]{2,1,0:T(8,128)S(1)} %shard_map.46) | data formatting | bytes 1572864

commit v2 on v0

v2 whole, which is shorter than its diff:
```python
import functools
import math

import jax
import jax.numpy as jnp
from jax import lax
from jax.experimental import pallas as pl
from jax.experimental.pallas import tpu as pltpu
from jax.sharding import PartitionSpec as P

CONTRIB = 128
SUB = 512
GROUP = 4
CHUNK = 512
ROWS = 256
STEP = SUB // CONTRIB

MESH = pl.DeviceIdType.MESH

S, X, Y, D = (0, 0), (1, 0), (0, 1), (1, 1)
END_TURNS = (1, 3, 0, 2)
END_PLAN = (
    ((1, S),),
    ((1, X),),
    ((3, S), (0, S), (0, X), (0, Y), (0, D),),
    ((3, X), (3, Y),),
    ((3, D), (1, Y), (1, D), (2, S), (2, X), (2, Y), (2, D),),
)
INNER_TURNS = (2, 3, 0, 1)
INNER_PLAN = (
    ((2, S),),
    ((3, S), (2, X),),
    ((3, X), (3, Y),),
    ((3, D), (0, S), (0, X), (0, Y), (0, D), (2, Y), (2, D), (1, S), (1, X), (1, Y), (1, D),),
    (),
)


def sincos(turns, period):
    quarter = jnp.floor(turns.astype(jnp.float32) * (4.0 / period) + 0.5).astype(jnp.int32)
    rest = 4 * turns - quarter * period
    y = rest.astype(jnp.float32) * (0.5 * math.pi / period)
    z = y * y
    s = y + y * z * (-1.0 / 6 + z * (1.0 / 120 + z * (-1.0 / 5040 + z * (1.0 / 362880))))
    c = 1.0 + z * (-0.5 + z * (1.0 / 24 + z * (-1.0 / 720 + z * (1.0 / 40320))))
    odd = (quarter & 1) == 1
    cos_abs = jnp.where(odd, s, c)
    sin_abs = jnp.where(odd, c, s)
    cos_part = jnp.where(((quarter + 1) & 2) == 2, -cos_abs, cos_abs)
    sin_part = jnp.where((quarter & 2) == 2, -sin_abs, sin_abs)
    return cos_part, sin_part


def remainder(value, period):
    return value - jnp.floor(value.astype(jnp.float32) * (1.0 / period)).astype(jnp.int32) * period


def kernel(
    layers, facets, cols, width,
    slab_ref, window_ref, density_ref, offset_ref,
    out_ref,
    slab, counts, window_here, offset_here, wind, ca, sa, table, modulated, acc,
    send1, recv1, embed, kr, ki, rr, ri, raw,
    send2, recv2,
    ssem1, rsem1, ssem2, rsem2, csem, local_sem, reach_sem,
):
    layer = lax.axis_index("layer")
    me = lax.axis_index("facet")
    image = facets * width
    groups = facets // GROUP
    part = cols // layers
    band = layers * part
    mine = me // GROUP
    half = mine // (groups // 2)
    half_groups = groups // 2

    def ranked(step, end, inner):
        mirrored = jnp.where(half == 0, mine, groups - 1 - mine)
        g = jnp.where(mirrored == 0, end[0], inner[0])
        for i in range(1, groups):
            g = jnp.where(step == i, jnp.where(mirrored == 0, end[i], inner[i]), g)
        return jnp.where(half == 0, g, groups - 1 - g)

    def encode_order(step):
        if groups == 4:
            return ranked(step, END_TURNS, INNER_TURNS)
        return outward(step)

    def gather_order(step):
        if groups == 4:
            return ranked(step, (0, 1, 2, 3), (1, 0, 3, 2))
        return inward(step)

    def scatter_order(step):
        if groups == 4:
            return ranked(step, (3, 1, 2, 0), (3, 2, 0, 1))
        return outward(step)

    def adjoint_order(step):
        if groups == 4:
            return ranked(step, (0, 3, 1, 2), (0, 3, 1, 2))
        return inward(step)

    def outward(step):
        return jnp.where(
            half == 0,
            lax.rem(half_groups + step, groups),
            lax.rem(half_groups - 1 - step + groups, groups),
        )

    def inward(step):
        return jnp.where(half == 0, step, groups - 1 - step)

    def signal(sem, where):
        pl.semaphore_signal(sem, inc=1, device_id=where, device_id_type=MESH)

    near = [(layer, me ^ 2)] + [(lax.rem(layer + l, layers), me) for l in range(1, layers)]
    has_up = mine < groups - 1
    has_down = mine > 0

    barrier = pltpu.get_barrier_semaphore()
    signal(barrier, (layer, me ^ 1))
    for core in range(2):
        for there, f in near:
            signal(barrier, (there, f ^ core))

        @pl.when(has_up)
        def _():
            signal(barrier, (layer, (me + GROUP) ^ core))

        @pl.when(has_down)
        def _():
            signal(barrier, (layer, (me - GROUP) ^ core))

    fetch_offsets = pltpu.make_async_copy(offset_ref, offset_here, local_sem.at[2])
    fetch_offsets.start()
    fetch_window = pltpu.make_async_copy(window_ref, window_here, local_sem.at[1])
    fetch_window.start()
    fetch_slab = pltpu.make_async_copy(slab_ref, slab, local_sem.at[0])
    fetch_slab.start()

    def tell(reach):
        for where in near:
            signal(reach_sem.at[reach], where)

        @pl.when(has_up)
        def _():
            signal(reach_sem.at[reach], (layer, me + GROUP))

        @pl.when(has_down)
        def _():
            signal(reach_sem.at[reach], (layer, me - GROUP))

    def meet(reach):
        @pl.when(jnp.logical_and(has_up, has_down))
        def _():
            pl.semaphore_wait(reach_sem.at[reach], len(near) + 2)

        @pl.when(jnp.logical_not(jnp.logical_and(has_up, has_down)))
        def _():
            pl.semaphore_wait(reach_sem.at[reach], len(near) + 1)

    lane = lax.broadcasted_iota(jnp.int32, (ROWS, CONTRIB), 1) * STEP
    row = lax.broadcasted_iota(jnp.int32, (ROWS, CONTRIB), 0)
    base_c, base_s = sincos(remainder(lane * me, facets) * width + remainder(lane * row, image), image)
    small = lax.broadcasted_iota(jnp.int32, (8, CONTRIB), 1) * STEP
    for k in range(width // ROWS):
        rot_c, rot_s = sincos(remainder(small * (ROWS * k), image), image)
        rot_c = rot_c[0:1]
        rot_s = rot_s[0:1]
        table[k * ROWS:(k + 1) * ROWS, 0:CONTRIB] = (base_c * rot_c - base_s * rot_s).astype(jnp.bfloat16)
        table[k * ROWS:(k + 1) * ROWS, CONTRIB:2 * CONTRIB] = (
            base_c * rot_s + base_s * rot_c
        ).astype(jnp.bfloat16)

    fetch_offsets.wait()
    square = (GROUP * groups, GROUP * groups)
    on_diagonal = lax.broadcasted_iota(jnp.int32, square, 0) == lax.broadcasted_iota(jnp.int32, square, 1)
    offs = jnp.sum(
        jnp.where(on_diagonal, offset_here[...].astype(jnp.float32), 0.0), axis=1, keepdims=True
    ).astype(jnp.int32)
    start = remainder(offs * me, facets) * width
    cell = lax.broadcasted_iota(jnp.int32, (facets, width), 1)
    turns = start + remainder(offs * cell, image)
    cos_a, sin_a = sincos(turns, image)
    ca[...] = cos_a
    sa[...] = sin_a

    fetch_window.wait()
    fetch_slab.wait()
    window = window_here[...]
    for p in range(2):
        whole = (slab[0, p].astype(jnp.float32) * window).astype(jnp.bfloat16).astype(jnp.float32)
        wind[p * band:(p + 1) * band, :] = whole

    scale1 = width ** -0.5

    def deliver(h, s):
        pltpu.make_async_remote_copy(
            src_ref=send1.at[s * layers + h], dst_ref=recv1.at[me, layer],
            send_sem=ssem1, recv_sem=rsem1.at[mine],
            device_id=(h, s), device_id_type=MESH,
        ).start()

    def planned(turn):
        outer = jnp.logical_or(mine == 0, mine == groups - 1)
        for i in range(groups + 1):
            for at_end, plan in ((True, END_PLAN[i]), (False, INNER_PLAN[i])):
                if not plan:
                    continue

                @pl.when(jnp.logical_and(turn == i, outer if at_end else jnp.logical_not(outer)))
                def _():
                    for g, (dx, dl) in plan:
                        there = jnp.where(half == 0, g, groups - 1 - g)
                        straight = there * GROUP + lax.rem(me, GROUP)
                        home = g == (0 if at_end else 1) and not dx and not dl
                        for core in range(2):
                            if home and core == 0:
                                pltpu.make_async_copy(
                                    send1.at[me * layers + layer], recv1.at[me, layer], rsem1.at[mine]
                                ).start()
                            else:
                                deliver(layer ^ dl, straight ^ (2 * dx + core))

    def dispatch(turn):
        if groups == 4 and layers == 2:
            planned(turn)
            return

        def slot(a, carry):
            g = encode_order(a)
            ahead = jnp.abs(g - mine)
            straight = g * GROUP + lax.rem(me, GROUP)
            for off in range(3):
                reach = ahead + off
                late = jnp.logical_and(a < turn, reach == turn + 1)
                fresh = jnp.logical_and(a == turn, reach <= turn + 1)

                @pl.when(jnp.logical_or(late, fresh))
                def _():
                    if off == 0:
                        deliver(layer, straight ^ 1)

                        @pl.when(g != mine)
                        def _():
                            deliver(layer, straight)

                        @pl.when(g == mine)
                        def _():
                            pltpu.make_async_copy(
                                send1.at[me * layers + layer], recv1.at[me, layer], rsem1.at[mine]
                            ).start()

                    for core in range(2):
                        if off == 1:
                            deliver(layer, straight ^ (2 + core))
                        if off > 0:
                            for l in range(1, layers):
                                deliver(lax.rem(layer + l, layers), straight ^ (2 * off - 2 + core))

            return carry

        lax.fori_loop(0, groups, slot, 0)

    def encode(turn, carry):
        step = turn
        g = encode_order(step)
        for k in range(width // CHUNK):
            xs = slice(k * CHUNK, (k + 1) * CHUNK)
            for t in range(GROUP):
                s = g * GROUP + t
                c_row = ca[pl.ds(s, 1), xs]
                s_row = sa[pl.ds(s, 1), xs]
                wr = wind[0:band, xs]
                wi = wind[band:2 * band, xs]
                lo = t * 2 * band
                modulated[k % 2, lo:lo + band, :] = (wr * c_row + wi * s_row).astype(jnp.bfloat16)
                modulated[k % 2, lo + band:lo + 2 * band, :] = (wi * c_row - wr * s_row).astype(jnp.bfloat16)
            prod = jnp.dot(modulated[k % 2], table[xs, :], preferred_element_type=jnp.float32)
            if k == 0:
                acc[...] = prod
            else:
                acc[...] += prod
        for t in range(GROUP):
            lo = t * 2 * band
            pr = acc[lo:lo + band, :]
            pi = acc[lo + band:lo + 2 * band, :]
            real = (pr[:, :CONTRIB] + pi[:, CONTRIB:]) * scale1
            imag = (pi[:, :CONTRIB] - pr[:, CONTRIB:]) * scale1
            for h in range(layers):
                hs = slice(h * part, (h + 1) * part)
                send1[(g * GROUP + t) * layers + h] = jnp.concatenate([real[hs], imag[hs]], axis=0).astype(jnp.bfloat16)

        @pl.when(turn == 0)
        def _():
            both = jnp.logical_and(has_up, has_down)

            @pl.when(both)
            def _():
                pl.semaphore_wait(barrier, 1 + 2 * (len(near) + 2))

            @pl.when(jnp.logical_not(both))
            def _():
                pl.semaphore_wait(barrier, 1 + 2 * (len(near) + 1))

            tell(2)

        @pl.when(turn > 0)
        def _():
            meet(turn + 1)
            tell(turn + 2)

        dispatch(turn)

        @pl.when(turn == 0)
        def _():
            for l in range(layers):

                @pl.when(layer == l)
                def _():
                    pltpu.make_async_copy(
                        density_ref.at[0, l * part:(l + 1) * part], counts.at[l], csem.at[1]
                    ).start()

                @pl.when(layer != l)
                def _():
                    pltpu.make_async_remote_copy(
                        src_ref=density_ref.at[0, l * part:(l + 1) * part], dst_ref=counts.at[layer],
                        send_sem=csem.at[0], recv_sem=csem.at[1],
                        device_id=(l, me), device_id_type=MESH,
                    ).start()

        return carry

    lax.fori_loop(0, groups, encode, 0)
    meet(groups + 1)
    dispatch(groups)

    spacing = lax.broadcasted_iota(jnp.int32, (CONTRIB, SUB), 1) - STEP * lax.broadcasted_iota(
        jnp.int32, (CONTRIB, SUB), 0
    )
    scaled = spacing.astype(jnp.float32) * (1.0 / STEP)
    weight_k = 1.0 / (1.0 + scaled * scaled)
    c0, s0 = sincos(spacing, 2 * facets)
    kr[...] = c0 * weight_k
    ki[...] = s0 * weight_k
    c1, s1 = sincos(spacing, facets)
    rr[...] = c1
    ri[...] = s1

    def make_embed(f, carry):
        r = kr[...]
        i = ki[...]
        lo = pl.multiple_of(f * CONTRIB, CONTRIB)
        embed[pl.ds(lo, CONTRIB), 0:SUB] = r.astype(jnp.bfloat16)
        embed[pl.ds(lo, CONTRIB), SUB:2 * SUB] = (-i).astype(jnp.bfloat16)
        a = rr[...]
        b = ri[...]
        kr[...] = r * a - i * b
        ki[...] = r * b + i * a
        return carry

    lax.fori_loop(0, facets, make_embed, 0)

    pltpu.make_async_copy(counts, counts, csem.at[1]).wait()
    sub_scale = (2 * facets) ** -0.5
    dims = (((1,), (1,)), ((), ()))

    raw[...] = jnp.zeros_like(raw)

    def gather(step, inner):
        g = gather_order(step)
        piece = recv1.at[pl.ds(g * GROUP, GROUP)]
        pltpu.make_async_copy(piece, piece, rsem1.at[g]).wait()
        lhs = jnp.concatenate(
            [recv1[g * GROUP + t].reshape(2 * band, CONTRIB) for t in range(GROUP)], axis=1
        )
        lo = pl.multiple_of(g * GROUP * CONTRIB, GROUP * CONTRIB)
        raw[...] += jnp.dot(
            lhs, embed[pl.ds(lo, GROUP * CONTRIB), :], preferred_element_type=jnp.float32
        )
        return inner

    lax.fori_loop(0, groups, gather, 0)

    total_r = jnp.zeros((part, SUB), jnp.float32)
    total_i = jnp.zeros((part, SUB), jnp.float32)
    for l in range(layers):
        here = counts[l]
        weights = jnp.where(
            here > 0, 1.0 / jnp.maximum(here, 1).astype(jnp.float32), 0.0
        )
        re = slice(2 * l * part, (2 * l + 1) * part)
        im = slice((2 * l + 1) * part, (2 * l + 2) * part)
        raw_r = raw[re, 0:SUB] - raw[im, SUB:2 * SUB]
        raw_i = raw[re, SUB:2 * SUB] + raw[im, 0:SUB]
        total_r += (raw_r * weights * sub_scale).astype(jnp.bfloat16).astype(jnp.float32)
        total_i += (raw_i * weights * sub_scale).astype(jnp.bfloat16).astype(jnp.float32)
    gridded = jnp.concatenate([total_r, total_i], axis=0).astype(jnp.bfloat16)

    def scatter(step, inner):
        g = scatter_order(step)
        lo = pl.multiple_of(g * GROUP * CONTRIB, GROUP * CONTRIB)
        er = embed[pl.ds(lo, GROUP * CONTRIB), 0:SUB]
        ei = embed[pl.ds(lo, GROUP * CONTRIB), SUB:2 * SUB]
        pr = lax.dot_general(gridded, er, dims, preferred_element_type=jnp.float32)
        pi = lax.dot_general(gridded, ei, dims, preferred_element_type=jnp.float32)
        real = (pr[0:part] + pi[part:2 * part]) * 0.5
        imag = (pr[part:2 * part] - pi[0:part]) * 0.5
        both = jnp.concatenate([real, imag], axis=0).astype(jnp.bfloat16)
        for t in range(GROUP):
            send2[g * GROUP + t] = both[:, t * CONTRIB:(t + 1) * CONTRIB]
        for t in range(GROUP):
            f = g * GROUP + t

            @pl.when(f != me)
            def _():
                pltpu.make_async_remote_copy(
                    src_ref=send2.at[f], dst_ref=recv2.at[me],
                    send_sem=ssem2, recv_sem=rsem2.at[mine],
                    device_id=(layer, f), device_id_type=MESH,
                ).start()

            @pl.when(f == me)
            def _():
                pltpu.make_async_copy(send2.at[f], recv2.at[me], rsem2.at[mine]).start()

        return inner

    lax.fori_loop(0, groups, scatter, 0)

    out_ref[...] = jnp.zeros_like(out_ref)
    out_scale = (facets * CONTRIB) ** -0.5

    def adjoint(turn, carry):
        step = turn
        g = adjoint_order(step)
        piece = recv2.at[pl.ds(g * GROUP, GROUP)]
        pltpu.make_async_copy(piece, piece, rsem2.at[g]).wait()
        tops = []
        for t in range(GROUP):
            both = recv2[g * GROUP + t].astype(jnp.float32)
            br = both[0:part]
            bi = both[part:2 * part]
            tops.append(jnp.concatenate([br, -bi], axis=1))
            tops.append(jnp.concatenate([bi, br], axis=1))
        lhs = jnp.concatenate(tops, axis=0).astype(jnp.bfloat16)
        for k in range(width // CHUNK):
            xs = slice(k * CHUNK, (k + 1) * CHUNK)
            prod = lax.dot_general(lhs, table[xs, :], dims, preferred_element_type=jnp.float32)
            out_r = out_ref[0, :, xs]
            out_i = out_ref[1, :, xs]
            for t in range(GROUP):
                s = g * GROUP + t
                c_row = ca[pl.ds(s, 1), xs]
                s_row = sa[pl.ds(s, 1), xs]
                gr = prod[(2 * t) * part:(2 * t + 1) * part]
                gi = prod[(2 * t + 1) * part:(2 * t + 2) * part]
                out_r = out_r + (c_row * gr - s_row * gi)
                out_i = out_i + (c_row * gi + s_row * gr)
            factor = jnp.where(step == groups - 1, window_here[:, xs] * out_scale, 1.0)
            out_ref[0, :, xs] = out_r * factor
            out_ref[1, :, xs] = out_i * factor
        return carry

    lax.fori_loop(0, groups, adjoint, 0)

    for ref, sem in (
        (send1.at[pl.ds(0, facets * layers - 1)], ssem1),
        (send2.at[pl.ds(0, facets - 1)], ssem2),
        (counts.at[pl.ds(0, layers - 1)], csem.at[0]),
    ):
        pltpu.make_async_copy(ref, ref, sem).wait()


def shards(slabs, window, density, offsets):
    facets = lax.axis_size("facet")
    layers = lax.axis_size("layer")
    cols = slabs.shape[2]
    width = slabs.shape[3]
    part = cols // layers
    f32, bf16 = jnp.float32, jnp.bfloat16
    summed = pl.pallas_call(
        functools.partial(kernel, layers, facets, cols, width),
        out_shape=jax.ShapeDtypeStruct((2, part, width), f32),
        in_specs=[pl.BlockSpec(memory_space=pltpu.HBM)] * 4,
        out_specs=pl.BlockSpec(memory_space=pltpu.VMEM),
        scratch_shapes=[
            pltpu.VMEM(slabs.shape, bf16),
            pltpu.VMEM((layers, part, SUB), jnp.int32),
            pltpu.VMEM((1, width), f32),
            pltpu.VMEM((1, facets), jnp.int32),
            pltpu.VMEM((2 * layers * part, width), f32),
            pltpu.VMEM((facets, width), f32),
            pltpu.VMEM((facets, width), f32),
            pltpu.VMEM((width, 2 * CONTRIB), bf16),
            pltpu.VMEM((2, GROUP * 2 * layers * part, CHUNK), bf16),
            pltpu.VMEM((GROUP * 2 * layers * part, 2 * CONTRIB), f32),
            pltpu.VMEM((facets * layers, 2 * part, CONTRIB), bf16),
            pltpu.VMEM((facets, layers, 2 * part, CONTRIB), bf16),
            pltpu.VMEM((facets * CONTRIB, 2 * SUB), bf16),
            pltpu.VMEM((CONTRIB, SUB), f32),
            pltpu.VMEM((CONTRIB, SUB), f32),
            pltpu.VMEM((CONTRIB, SUB), f32),
            pltpu.VMEM((CONTRIB, SUB), f32),
            pltpu.VMEM((2 * layers * part, 2 * SUB), f32),
            pltpu.VMEM((facets, 2 * part, CONTRIB), bf16),
            pltpu.VMEM((facets, 2 * part, CONTRIB), bf16),
            pltpu.SemaphoreType.DMA,
            pltpu.SemaphoreType.DMA((facets // GROUP,)),
            pltpu.SemaphoreType.DMA,
            pltpu.SemaphoreType.DMA((facets // GROUP,)),
            pltpu.SemaphoreType.DMA((2,)),
            pltpu.SemaphoreType.DMA((3,)),
            pltpu.SemaphoreType.REGULAR((facets // GROUP + 2,)),
        ],
        compiler_params=pltpu.CompilerParams(
            collective_id=0, has_side_effects=True, vmem_limit_bytes=(14 + facets) * 1024 * 1024
        ),
    )(
        *(
            pltpu.with_memory_space_constraint(x, pltpu.HBM)
            for x in (slabs, window[None, :], density, offsets[None, :])
        )
    )
    return summed


def solution(mesh):
    placed = (P("layer", None, None, "facet"), P("facet"), P("layer", None, "facet"), P())
    return jax.shard_map(
        shards, mesh=mesh, in_specs=placed, out_specs=P(None, "layer", "facet"), check_vma=False
    )
```

time: 35.1 us -> 29.7 us (0.85)
  Pallas kernels: 34 us -> 28.6 us
    pallas_call x1, Pallas kernels: 34 us -> 28.6 us  [shards(): pl.pallas_call(functools.partial(kernel, layers, facets, cols, width), ou...]
where the time goes in v2:
time: 29.7 us; the launch traced here: 29.5 us
  Pallas kernels  28.6 us (96%)
  local copies, waits for them, and re-layouts  0.88 us (3%)
    pallas_call x1, Pallas kernels, shards(): pl.pallas_call(functools.partial(kernel, layers, facets, cols, width), ou...  28.6 us
    unnamed x1, local copies, waits for them, and re-layouts  0.88 us

profile of v2, /device:TPU:0, one launch (start us, length us, event | category | flops | bytes accessed | tf_op | source)
XLA Modules:
  0.0 29.5 jit_solution(3146747212238486235)
XLA Ops:
  0.0 28.6 %shard_map.46 = f32[2,32,3072]{2,1,0:T(8,128)S(1)} custom-call(bf16[1,2,64,3072]{3,2,1,0:T(8,128)(2,1)} %slab_ref.1, f32[1,3072]{1,0:T(1,128)} %bitcast.2, s32[1,64,512]{2,1,0:T(8,128)} %density_ref.1, s32[1,16]{1,0:T(1,128)} %bitcast.3), custom_call_target="tpu_custom_call" | custom-call | tf_op jit(solution)/shard_map/pallas_call | solution.py:484
  28.6 0.9 %copy.6 = f32[2,32,3072]{2,1,0:T(8,128)} copy(f32[2,32,3072]{2,1,0:T(8,128)S(1)} %shard_map.46) | data formatting | bytes 1572864

commit v3 on v2

--- a/solution.py
+++ b/solution.py
@@ -13,6 +13,7 @@
 GROUP = 4
 CHUNK = 512
 ROWS = 256
+TILES = 8
 STEP = SUB // CONTRIB
 
 MESH = pl.DeviceIdType.MESH
@@ -61,7 +62,7 @@
     out_ref,
     slab, counts, window_here, offset_here, wind, ca, sa, table, modulated, acc,
     send1, recv1, embed, kr, ki, rr, ri, raw,
-    send2, recv2,
+    send2, recv2, offs_wide, fine, phase_c, phase_s, turned, total,
     ssem1, rsem1, ssem2, rsem2, csem, local_sem, reach_sem,
 ):
     layer = lax.axis_index("layer")
@@ -93,12 +94,12 @@
 
     def scatter_order(step):
         if groups == 4:
-            return ranked(step, (3, 1, 2, 0), (3, 2, 0, 1))
+            return ranked(step, (3, 0, 1, 2), (0, 1, 3, 2))
         return outward(step)
 
     def adjoint_order(step):
         if groups == 4:
-            return ranked(step, (0, 3, 1, 2), (0, 3, 1, 2))
+            return ranked(step, (0, 3, 2, 1), (1, 0, 3, 2))
         return inward(step)
 
     def outward(step):
@@ -179,6 +180,7 @@
     offs = jnp.sum(
         jnp.where(on_diagonal, offset_here[...].astype(jnp.float32), 0.0), axis=1, keepdims=True
     ).astype(jnp.int32)
+    offs_wide[...] = jnp.broadcast_to(offs, offs_wide.shape)
     start = remainder(offs * me, facets) * width
     cell = lax.broadcasted_iota(jnp.int32, (facets, width), 1)
     turns = start + remainder(offs * cell, image)
@@ -363,6 +365,38 @@
 
     lax.fori_loop(0, facets, make_embed, 0)
 
+    tiles = width // CONTRIB
+    square = (CONTRIB, CONTRIB)
+    lane_here = lax.broadcasted_iota(jnp.int32, square, 1)
+    fine_c, fine_s = sincos(
+        remainder(STEP * lax.broadcasted_iota(jnp.int32, square, 0) * lane_here, image), image
+    )
+    kr[:, 0:CONTRIB] = fine_c
+    ki[:, 0:CONTRIB] = fine_s
+    coarse = CONTRIB * lax.broadcasted_iota(jnp.int32, (tiles, CONTRIB), 0)
+    steps = STEP * lax.broadcasted_iota(jnp.int32, (tiles, CONTRIB), 1)
+
+    def make_phases(f, carry):
+        off = offs_wide[pl.ds(f, 1), :]
+        c, i = sincos(remainder(off * lane_here[0:1], image), image)
+        fc = kr[:, 0:CONTRIB] * c - ki[:, 0:CONTRIB] * i
+        fs = kr[:, 0:CONTRIB] * i + ki[:, 0:CONTRIB] * c
+        lo = pl.multiple_of(f * 2 * CONTRIB, 2 * CONTRIB)
+        fine[pl.ds(lo, CONTRIB), 0:CONTRIB] = fc.astype(jnp.bfloat16)
+        fine[pl.ds(lo, CONTRIB), CONTRIB:2 * CONTRIB] = fs.astype(jnp.bfloat16)
+        fine[pl.ds(lo + CONTRIB, CONTRIB), 0:CONTRIB] = (-fs).astype(jnp.bfloat16)
+        fine[pl.ds(lo + CONTRIB, CONTRIB), CONTRIB:2 * CONTRIB] = fc.astype(jnp.bfloat16)
+        frequency = off + steps
+        pc, ps = sincos(
+            remainder(frequency * me, facets) * width + remainder(frequency * coarse, image), image
+        )
+        phase_c[f] = pc
+        phase_s[f] = ps
+        return carry
+
+    lax.fori_loop(0, facets, make_phases, 0)
+    total[...] = jnp.zeros_like(total)
+
     pltpu.make_async_copy(counts, counts, csem.at[1]).wait()
     sub_scale = (2 * facets) ** -0.5
     dims = (((1,), (1,)), ((), ()))
@@ -397,18 +431,21 @@
         raw_i = raw[re, SUB:2 * SUB] + raw[im, 0:SUB]
         total_r += (raw_r * weights * sub_scale).astype(jnp.bfloat16).astype(jnp.float32)
         total_i += (raw_i * weights * sub_scale).astype(jnp.bfloat16).astype(jnp.float32)
-    gridded = jnp.concatenate([total_r, total_i], axis=0).astype(jnp.bfloat16)
+    gridded = jnp.concatenate(
+        [
+            jnp.concatenate([total_r, total_i], axis=1),
+            jnp.concatenate([total_i, -total_r], axis=1),
+        ],
+        axis=0,
+    ).astype(jnp.bfloat16)
 
     def scatter(step, inner):
         g = scatter_order(step)
         lo = pl.multiple_of(g * GROUP * CONTRIB, GROUP * CONTRIB)
-        er = embed[pl.ds(lo, GROUP * CONTRIB), 0:SUB]
-        ei = embed[pl.ds(lo, GROUP * CONTRIB), SUB:2 * SUB]
-        pr = lax.dot_general(gridded, er, dims, preferred_element_type=jnp.float32)
-        pi = lax.dot_general(gridded, ei, dims, preferred_element_type=jnp.float32)
-        real = (pr[0:part] + pi[part:2 * part]) * 0.5
-        imag = (pr[part:2 * part] - pi[0:part]) * 0.5
-        both = jnp.concatenate([real, imag], axis=0).astype(jnp.bfloat16)
+        back = lax.dot_general(
+            gridded, embed[pl.ds(lo, GROUP * CONTRIB), :], dims, preferred_element_type=jnp.float32
+        )
+        both = (back * 0.5).astype(jnp.bfloat16)
         for t in range(GROUP):
             send2[g * GROUP + t] = both[:, t * CONTRIB:(t + 1) * CONTRIB]
         for t in range(GROUP):
@@ -430,41 +467,47 @@
 
     lax.fori_loop(0, groups, scatter, 0)
 
-    out_ref[...] = jnp.zeros_like(out_ref)
     out_scale = (facets * CONTRIB) ** -0.5
 
-    def adjoint(turn, carry):
-        step = turn
+    def adjoint(step, last):
         g = adjoint_order(step)
         piece = recv2.at[pl.ds(g * GROUP, GROUP)]
         pltpu.make_async_copy(piece, piece, rsem2.at[g]).wait()
-        tops = []
-        for t in range(GROUP):
-            both = recv2[g * GROUP + t].astype(jnp.float32)
-            br = both[0:part]
-            bi = both[part:2 * part]
-            tops.append(jnp.concatenate([br, -bi], axis=1))
-            tops.append(jnp.concatenate([bi, br], axis=1))
-        lhs = jnp.concatenate(tops, axis=0).astype(jnp.bfloat16)
-        for k in range(width // CHUNK):
-            xs = slice(k * CHUNK, (k + 1) * CHUNK)
-            prod = lax.dot_general(lhs, table[xs, :], dims, preferred_element_type=jnp.float32)
-            out_r = out_ref[0, :, xs]
-            out_i = out_ref[1, :, xs]
+        lo = pl.multiple_of(g * GROUP * 2 * CONTRIB, GROUP * 2 * CONTRIB)
+        for k in range(tiles // TILES):
+            lhs = []
             for t in range(GROUP):
-                s = g * GROUP + t
-                c_row = ca[pl.ds(s, 1), xs]
-                s_row = sa[pl.ds(s, 1), xs]
-                gr = prod[(2 * t) * part:(2 * t + 1) * part]
-                gi = prod[(2 * t + 1) * part:(2 * t + 2) * part]
-                out_r = out_r + (c_row * gr - s_row * gi)
-                out_i = out_i + (c_row * gi + s_row * gr)
-            factor = jnp.where(step == groups - 1, window_here[:, xs] * out_scale, 1.0)
-            out_ref[0, :, xs] = out_r * factor
-            out_ref[1, :, xs] = out_i * factor
+                both = recv2[g * GROUP + t].astype(jnp.float32)
+                br = both[0:part]
+                bi = both[part:2 * part]
+                turned_r = []
+                turned_i = []
+                for i in range(TILES):
+                    pc = phase_c[g * GROUP + t, k * TILES + i:k * TILES + i + 1, :]
+                    ps = phase_s[g * GROUP + t, k * TILES + i:k * TILES + i + 1, :]
+                    turned_r.append(br * pc - bi * ps)
+                    turned_i.append(br * ps + bi * pc)
+                lhs.append(jnp.concatenate(turned_r, axis=0).astype(jnp.bfloat16))
+                lhs.append(jnp.concatenate(turned_i, axis=0).astype(jnp.bfloat16))
+            rows = slice(k * TILES * part, (k + 1) * TILES * part)
+            new = total[rows, :] + jnp.dot(
+                jnp.concatenate(lhs, axis=1), fine[pl.ds(lo, GROUP * 2 * CONTRIB), :], preferred_element_type=jnp.float32
+            )
+            if not last:
+                total[rows, :] = new
+                continue
+            for i in range(TILES):
+                xs = slice((k * TILES + i) * CONTRIB, (k * TILES + i + 1) * CONTRIB)
+                factor = window_here[:, xs] * out_scale
+                out_ref[0, :, xs] = new[i * part:(i + 1) * part, 0:CONTRIB] * factor
+                out_ref[1, :, xs] = new[i * part:(i + 1) * part, CONTRIB:2 * CONTRIB] * factor
+
+    def early(step, carry):
+        adjoint(step, False)
         return carry
 
-    lax.fori_loop(0, groups, adjoint, 0)
+    lax.fori_loop(0, groups - 1, early, 0)
+    adjoint(groups - 1, True)
 
     for ref, sem in (
         (send1.at[pl.ds(0, facets * layers - 1)], ssem1),
@@ -507,6 +550,12 @@
             pltpu.VMEM((2 * layers * part, 2 * SUB), f32),
             pltpu.VMEM((facets, 2 * part, CONTRIB), bf16),
             pltpu.VMEM((facets, 2 * part, CONTRIB), bf16),
+            pltpu.VMEM((facets, CONTRIB), jnp.int32),
+            pltpu.VMEM((facets * 2 * CONTRIB, 2 * CONTRIB), bf16),
+            pltpu.VMEM((facets, width // CONTRIB, CONTRIB), f32),
+            pltpu.VMEM((facets, width // CONTRIB, CONTRIB), f32),
+            pltpu.VMEM((2, TILES * part, GROUP * 2 * CONTRIB), bf16),
+            pltpu.VMEM((width // CONTRIB * part, 2 * CONTRIB), f32),
             pltpu.SemaphoreType.DMA,
             pltpu.SemaphoreType.DMA((facets // GROUP,)),
             pltpu.SemaphoreType.DMA,

time: 29.7 us -> 29 us (0.976)
  Pallas kernels: 28.6 us -> 27.7 us
    pallas_call x1, Pallas kernels: 28.6 us -> 27.7 us  [shards(): pl.pallas_call(functools.partial(kernel, layers, facets, cols, width), ou...]
where the time goes in v3:
time: 29 us; the launch traced here: 28.6 us
  Pallas kernels  27.7 us (96%)
  local copies, waits for them, and re-layouts  0.88 us (3%)
    pallas_call x1, Pallas kernels, shards(): pl.pallas_call(functools.partial(kernel, layers, facets, cols, width), ou...  27.7 us
    unnamed x1, local copies, waits for them, and re-layouts  0.88 us

profile of v3, /device:TPU:0, one launch (start us, length us, event | category | flops | bytes accessed | tf_op | source)
XLA Modules:
  0.0 28.6 jit_solution(2263054279553712111)
XLA Ops:
  0.0 27.7 %shard_map.46 = f32[2,32,3072]{2,1,0:T(8,128)S(1)} custom-call(bf16[1,2,64,3072]{3,2,1,0:T(8,128)(2,1)} %slab_ref.1, f32[1,3072]{1,0:T(1,128)} %bitcast.2, s32[1,64,512]{2,1,0:T(8,128)} %density_ref.1, s32[1,16]{1,0:T(1,128)} %bitcast.3), custom_call_target="tpu_custom_call" | custom-call | tf_op jit(solution)/shard_map/pallas_call | solution.py:527
  27.7 0.9 %copy.6 = f32[2,32,3072]{2,1,0:T(8,128)} copy(f32[2,32,3072]{2,1,0:T(8,128)S(1)} %shard_map.46) | data formatting | bytes 1572864

commit v4 on v3

--- a/solution.py
+++ b/solution.py
@@ -14,6 +14,7 @@
 CHUNK = 512
 ROWS = 256
 TILES = 8
+PAIR = GROUP // 2
 STEP = SUB // CONTRIB
 
 MESH = pl.DeviceIdType.MESH
@@ -62,7 +63,7 @@
     out_ref,
     slab, counts, window_here, offset_here, wind, ca, sa, table, modulated, acc,
     send1, recv1, embed, kr, ki, rr, ri, raw,
-    send2, recv2, offs_wide, fine, phase_c, phase_s, turned, total,
+    send2, recv2, offs_wide, fine, phase_c, phase_s, turned, total, weighting,
     ssem1, rsem1, ssem2, rsem2, csem, local_sem, reach_sem,
 ):
     layer = lax.axis_index("layer")
@@ -161,14 +162,24 @@
         def _():
             pl.semaphore_wait(reach_sem.at[reach], len(near) + 1)
 
-    lane = lax.broadcasted_iota(jnp.int32, (ROWS, CONTRIB), 1) * STEP
-    row = lax.broadcasted_iota(jnp.int32, (ROWS, CONTRIB), 0)
-    base_c, base_s = sincos(remainder(lane * me, facets) * width + remainder(lane * row, image), image)
-    small = lax.broadcasted_iota(jnp.int32, (8, CONTRIB), 1) * STEP
+    def spread_rows(count, stride):
+        lane = lax.broadcasted_iota(jnp.int32, (count, CONTRIB), 1) * STEP
+        row = lax.broadcasted_iota(jnp.int32, (count, CONTRIB), 0) * stride
+        return lane, remainder(lane * row, image)
+
+    lane, turns = spread_rows(8, 1)
+    low_c, low_s = sincos(remainder(lane * me, facets) * width + turns, image)
+    mid_c, mid_s = sincos(spread_rows(ROWS // 8, 8)[1], image)
+    high_c, high_s = sincos(spread_rows(-(-width // ROWS // 8) * 8, ROWS)[1], image)
+    base_c = jnp.concatenate(
+        [low_c * mid_c[i:i + 1] - low_s * mid_s[i:i + 1] for i in range(ROWS // 8)], axis=0
+    )
+    base_s = jnp.concatenate(
+        [low_c * mid_s[i:i + 1] + low_s * mid_c[i:i + 1] for i in range(ROWS // 8)], axis=0
+    )
     for k in range(width // ROWS):
-        rot_c, rot_s = sincos(remainder(small * (ROWS * k), image), image)
-        rot_c = rot_c[0:1]
-        rot_s = rot_s[0:1]
+        rot_c = high_c[k:k + 1]
+        rot_s = high_s[k:k + 1]
         table[k * ROWS:(k + 1) * ROWS, 0:CONTRIB] = (base_c * rot_c - base_s * rot_s).astype(jnp.bfloat16)
         table[k * ROWS:(k + 1) * ROWS, CONTRIB:2 * CONTRIB] = (
             base_c * rot_s + base_s * rot_c
@@ -181,12 +192,18 @@
         jnp.where(on_diagonal, offset_here[...].astype(jnp.float32), 0.0), axis=1, keepdims=True
     ).astype(jnp.int32)
     offs_wide[...] = jnp.broadcast_to(offs, offs_wide.shape)
-    start = remainder(offs * me, facets) * width
-    cell = lax.broadcasted_iota(jnp.int32, (facets, width), 1)
-    turns = start + remainder(offs * cell, image)
-    cos_a, sin_a = sincos(turns, image)
-    ca[...] = cos_a
-    sa[...] = sin_a
+    cell = lax.broadcasted_iota(jnp.int32, (facets, CONTRIB), 1)
+    tile = jnp.minimum(cell, width // CONTRIB - 1) * CONTRIB
+    within_c, within_s = sincos(remainder(offs * cell, image), image)
+    tile_c, tile_s = sincos(
+        remainder(offs * me, facets) * width + remainder(offs * tile, image), image
+    )
+    for k in range(width // CONTRIB):
+        at_c = tile_c[:, k:k + 1]
+        at_s = tile_s[:, k:k + 1]
+        xs = slice(k * CONTRIB, (k + 1) * CONTRIB)
+        ca[:, xs] = within_c * at_c - within_s * at_s
+        sa[:, xs] = within_c * at_s + within_s * at_c
 
     fetch_window.wait()
     fetch_slab.wait()
@@ -401,6 +418,11 @@
     sub_scale = (2 * facets) ** -0.5
     dims = (((1,), (1,)), ((), ()))
 
+    for l in range(layers):
+        here = counts[l]
+        weighting[l] = jnp.where(
+            here > 0, 1.0 / jnp.maximum(here, 1).astype(jnp.float32), 0.0
+        ) * sub_scale
     raw[...] = jnp.zeros_like(raw)
 
     def gather(step, inner):
@@ -421,16 +443,13 @@
     total_r = jnp.zeros((part, SUB), jnp.float32)
     total_i = jnp.zeros((part, SUB), jnp.float32)
     for l in range(layers):
-        here = counts[l]
-        weights = jnp.where(
-            here > 0, 1.0 / jnp.maximum(here, 1).astype(jnp.float32), 0.0
-        )
+        weights = weighting[l]
         re = slice(2 * l * part, (2 * l + 1) * part)
         im = slice((2 * l + 1) * part, (2 * l + 2) * part)
         raw_r = raw[re, 0:SUB] - raw[im, SUB:2 * SUB]
         raw_i = raw[re, SUB:2 * SUB] + raw[im, 0:SUB]
-        total_r += (raw_r * weights * sub_scale).astype(jnp.bfloat16).astype(jnp.float32)
-        total_i += (raw_i * weights * sub_scale).astype(jnp.bfloat16).astype(jnp.float32)
+        total_r += (raw_r * weights).astype(jnp.bfloat16).astype(jnp.float32)
+        total_i += (raw_i * weights).astype(jnp.bfloat16).astype(jnp.float32)
     gridded = jnp.concatenate(
         [
             jnp.concatenate([total_r, total_i], axis=1),
@@ -439,17 +458,17 @@
         axis=0,
     ).astype(jnp.bfloat16)
 
-    def scatter(step, inner):
-        g = scatter_order(step)
-        lo = pl.multiple_of(g * GROUP * CONTRIB, GROUP * CONTRIB)
+    def scatter(turn, inner):
+        first = scatter_order(turn // 2) * GROUP + lax.rem(turn, 2) * PAIR
+        lo = pl.multiple_of(first * CONTRIB, PAIR * CONTRIB)
         back = lax.dot_general(
-            gridded, embed[pl.ds(lo, GROUP * CONTRIB), :], dims, preferred_element_type=jnp.float32
+            gridded, embed[pl.ds(lo, PAIR * CONTRIB), :], dims, preferred_element_type=jnp.float32
         )
         both = (back * 0.5).astype(jnp.bfloat16)
-        for t in range(GROUP):
-            send2[g * GROUP + t] = both[:, t * CONTRIB:(t + 1) * CONTRIB]
-        for t in range(GROUP):
-            f = g * GROUP + t
+        for t in range(PAIR):
+            send2[first + t] = both[:, t * CONTRIB:(t + 1) * CONTRIB]
+        for t in range(PAIR):
+            f = first + t
 
             @pl.when(f != me)
             def _():
@@ -465,7 +484,7 @@
 
         return inner
 
-    lax.fori_loop(0, groups, scatter, 0)
+    lax.fori_loop(0, 2 * groups, scatter, 0)
 
     out_scale = (facets * CONTRIB) ** -0.5
 
@@ -556,6 +575,7 @@
             pltpu.VMEM((facets, width // CONTRIB, CONTRIB), f32),
             pltpu.VMEM((2, TILES * part, GROUP * 2 * CONTRIB), bf16),
             pltpu.VMEM((width // CONTRIB * part, 2 * CONTRIB), f32),
+            pltpu.VMEM((layers, part, SUB), f32),
             pltpu.SemaphoreType.DMA,
             pltpu.SemaphoreType.DMA((facets // GROUP,)),
             pltpu.SemaphoreType.DMA,

time: 29 us -> 28.7 us (0.990)
  Pallas kernels: 27.7 us -> 27.4 us
where the time goes in v4:
time: 28.7 us; the launch traced here: 28.3 us
  Pallas kernels  27.4 us (95%)
  local copies, waits for them, and re-layouts  0.88 us (3%)
    pallas_call x1, Pallas kernels, shards(): pl.pallas_call(functools.partial(kernel, layers, facets, cols, width), ou...  27.4 us
    unnamed x1, local copies, waits for them, and re-layouts  0.88 us

profile of v4, /device:TPU:0, one launch (start us, length us, event | category | flops | bytes accessed | tf_op | source)
XLA Modules:
  0.0 28.3 jit_solution(12183337697215894358)
XLA Ops:
  0.0 27.4 %shard_map.46 = f32[2,32,3072]{2,1,0:T(8,128)S(1)} custom-call(bf16[1,2,64,3072]{3,2,1,0:T(8,128)(2,1)} %slab_ref.1, f32[1,3072]{1,0:T(1,128)} %bitcast.2, s32[1,64,512]{2,1,0:T(8,128)} %density_ref.1, s32[1,16]{1,0:T(1,128)} %bitcast.3), custom_call_target="tpu_custom_call" | custom-call | tf_op jit(solution)/shard_map/pallas_call | solution.py:546
  27.5 0.9 %copy.6 = f32[2,32,3072]{2,1,0:T(8,128)} copy(f32[2,32,3072]{2,1,0:T(8,128)S(1)} %shard_map.46) | data formatting | bytes 1572864

commit v5 on v4

--- a/solution.py
+++ b/solution.py
@@ -287,16 +287,18 @@
         g = encode_order(step)
         for k in range(width // CHUNK):
             xs = slice(k * CHUNK, (k + 1) * CHUNK)
+            rows = []
             for t in range(GROUP):
                 s = g * GROUP + t
                 c_row = ca[pl.ds(s, 1), xs]
                 s_row = sa[pl.ds(s, 1), xs]
                 wr = wind[0:band, xs]
                 wi = wind[band:2 * band, xs]
-                lo = t * 2 * band
-                modulated[k % 2, lo:lo + band, :] = (wr * c_row + wi * s_row).astype(jnp.bfloat16)
-                modulated[k % 2, lo + band:lo + 2 * band, :] = (wi * c_row - wr * s_row).astype(jnp.bfloat16)
-            prod = jnp.dot(modulated[k % 2], table[xs, :], preferred_element_type=jnp.float32)
+                rows.append((wr * c_row + wi * s_row).astype(jnp.bfloat16))
+                rows.append((wi * c_row - wr * s_row).astype(jnp.bfloat16))
+            prod = jnp.dot(
+                jnp.concatenate(rows, axis=0), table[xs, :], preferred_element_type=jnp.float32
+            )
             if k == 0:
                 acc[...] = prod
             else:

time: 28.7 us -> 28.7 us (level)
  no operation moved by 1% of the time
where the time goes in v5:
time: 28.7 us; the launch traced here: 28.3 us
  Pallas kernels  27.4 us (95%)
  local copies, waits for them, and re-layouts  0.88 us (3%)
    pallas_call x1, Pallas kernels, shards(): pl.pallas_call(functools.partial(kernel, layers, facets, cols, width), ou...  27.4 us
    unnamed x1, local copies, waits for them, and re-layouts  0.88 us

profile of v5, /device:TPU:0, one launch (start us, length us, event | category | flops | bytes accessed | tf_op | source)
XLA Modules:
  0.0 28.3 jit_solution(9923219722011497713)
XLA Ops:
  0.0 27.4 %shard_map.46 = f32[2,32,3072]{2,1,0:T(8,128)S(1)} custom-call(bf16[1,2,64,3072]{3,2,1,0:T(8,128)(2,1)} %slab_ref.1, f32[1,3072]{1,0:T(1,128)} %bitcast.2, s32[1,64,512]{2,1,0:T(8,128)} %density_ref.1, s32[1,16]{1,0:T(1,128)} %bitcast.3), custom_call_target="tpu_custom_call" | custom-call | tf_op jit(solution)/shard_map/pallas_call | solution.py:548
  27.4 0.9 %copy.6 = f32[2,32,3072]{2,1,0:T(8,128)} copy(f32[2,32,3072]{2,1,0:T(8,128)S(1)} %shard_map.46) | data formatting | bytes 1572864
